TPU v7x, 32 devices: a whole 2x2x4 slice. The times are simulated.
32 devices in a mesh: row: 16 (over z, y, core), col: 2 (over x).
Axes of the slice: x: 2, y: 2, z: 4, core: 2. Of those that a mesh axis runs over, the one named last changes fastest.
Arguments:
- start_block: float32 [4096, 256], P(('row', 'col')), may hold values from -6 to 6
- tiles: bfloat16 [16, 2, 14, 128, 128], P('row', 'col'), may hold values from -0.125 to 0.125
- tile_rows: int32 [16, 2, 14], P('row', 'col'), may hold values from -1 to 31, as said below
- tile_cols: int32 [16, 2, 14], P('row', 'col'), may hold values from -1 to 31, as said below
- bounds: float32 [3], replicated, may hold values from -2.6 to 2.6, as said below
Outputs:
- filtered: float32 [4096, 256], P(('row', 'col'))
Inputs may be any that keep to these rules, and one draw needn't show every extreme that they name: Vector rows form blocks of 128 rows, one block a device, in row+col order. On the device at grid row r and grid column c, a live slot names a block row held by one of the devices (r, any column) and a block column held by one of the devices (any row, c). Live slots come first; each device has 1 to 14 live slots, and one device has exactly 14 in every draw. No block position is named twice, and the mirror of a named position is never named unless it lies on the diagonal. tile_rows and tile_cols are -1 together. `tile_cols`: same slots as tile_rows. bounds[0] < bounds[1] < bounds[2].
All inputs are finite; a program needn't handle non-finite values.
Results may differ from a plain program's by a relative error of at most 0.0042.
Values may be sent and summed in bfloat16 or wider, within the bound.
A program may use at most 64 MiB of HBM per device.

v0:
```python
import jax
import jax.numpy as jnp
from jax import lax
from jax.sharding import PartitionSpec as P

DEGREE = 4


def local(start_block, tiles, tile_rows, tile_cols, bounds):
    rows_dev, vec_width = start_block.shape
    tile_size = tiles.shape[-1]
    blocks = rows_dev // tile_size
    row_count = lax.axis_size("row")
    col_count = lax.axis_size("col")
    near_count = col_count * blocks
    far_count = row_count * blocks
    row_index = lax.axis_index("row")
    col_index = lax.axis_index("col")
    slots = tiles.shape[2]
    tile_mats = tiles.reshape(slots, tile_size, tile_size)
    glob_rows = tile_rows.reshape(slots)
    glob_cols = tile_cols.reshape(slots)
    is_live = glob_rows >= 0
    local_rows = jnp.where(is_live, glob_rows - row_index * near_count, -1)
    local_cols = jnp.where(
        is_live, glob_cols // blocks // col_count * blocks + glob_cols % blocks, -1
    )
    slot_place = jnp.where(is_live, local_rows * far_count + local_cols, near_count * far_count)
    owned = jnp.zeros((near_count * far_count, tile_size, tile_size), jnp.bfloat16)
    owned = owned.at[slot_place].add(tile_mats, mode="drop")
    owned = owned.reshape(col_count, blocks, row_count, blocks, tile_size, tile_size)
    received = lax.all_to_all(
        lax.all_to_all(owned, "row", split_axis=2, concat_axis=2, tiled=True),
        "col",
        split_axis=0,
        concat_axis=0,
        tiled=True,
    )
    mirror = jnp.transpose(received, (0, 3, 2, 1, 5, 4))
    grid_shape = (col_count, blocks, row_count, blocks)
    col_grid = lax.broadcasted_iota(jnp.int32, grid_shape, 0)
    first_sub = lax.broadcasted_iota(jnp.int32, grid_shape, 1)
    row_grid = lax.broadcasted_iota(jnp.int32, grid_shape, 2)
    second_sub = lax.broadcasted_iota(jnp.int32, grid_shape, 3)
    on_diagonal = (col_grid == col_index) & (row_grid == row_index) & (first_sub == second_sub)
    zero_tile = jnp.zeros((), jnp.bfloat16)
    window = (jnp.where(on_diagonal[..., None, None], zero_tile, owned) + mirror).reshape(
        near_count, far_count, tile_size, tile_size
    )
    owned_here = lax.dynamic_index_in_dim(owned, col_index, 0, keepdims=False)
    owned_here = lax.dynamic_index_in_dim(owned_here, row_index, 1, keepdims=False)
    block_ids = jnp.arange(blocks)
    diagonal_tiles = owned_here[block_ids, block_ids]

    def apply_matrix(vectors):
        low_vectors = vectors.astype(jnp.bfloat16)
        far_vectors = lax.all_gather(low_vectors, "row", axis=0, tiled=True).reshape(
            far_count, tile_size, vec_width
        )
        near_partial = jnp.einsum(
            "apxy,pyk->axk", window, far_vectors, preferred_element_type=jnp.float32
        )
        own_vectors = lax.dynamic_slice_in_dim(far_vectors, row_index * blocks, blocks, 0)
        diagonal_part = jnp.einsum(
            "uxy,uyk->uxk", diagonal_tiles, own_vectors, preferred_element_type=jnp.float32
        )
        current_rows = lax.dynamic_slice_in_dim(near_partial, col_index * blocks, blocks, 0)
        near_partial = lax.dynamic_update_slice_in_dim(
            near_partial, current_rows + diagonal_part, col_index * blocks, 0
        )
        combined = lax.psum_scatter(
            near_partial.reshape(near_count * tile_size, vec_width),
            "col",
            scatter_dimension=0,
            tiled=True,
        )
        return combined

    half_width = (bounds[2] - bounds[1]) * 0.5
    center = (bounds[2] + bounds[1]) * 0.5
    sigma_one = half_width / (bounds[0] - center)
    previous = start_block
    current = (apply_matrix(start_block) - center * start_block) * (sigma_one / half_width)
    sigma = sigma_one
    for turn_index in range(DEGREE - 1):
        sigma_next = 1.0 / (2.0 / sigma_one - sigma)
        product = apply_matrix(current)
        following = (product - center * current) * (
            2.0 * sigma_next / half_width
        ) - sigma * sigma_next * previous
        previous = current
        current = following
        sigma = sigma_next
    return current


def solution(mesh):
    placed = (
        P(("row", "col"), None),
        P("row", "col", None, None, None),
        P("row", "col", None),
        P("row", "col", None),
        P(),
    )
    return jax.shard_map(
        local, mesh=mesh, in_specs=placed, out_specs=P(("row", "col"), None), check_vma=False
    )
```

profile of v0, /device:TPU:0, one launch (start us, length us, event | category | flops | bytes accessed | tf_op | source)
XLA Modules:
  0.0 251.6 jit_solution(16781734857981256183)
XLA Ops:
  6.5 0.7 copy-done.8
  7.2 0.0 copy-done.9
  7.2 0.0 copy-start.6
  7.2 0.2 broadcast_in_dim.27
  7.5 0.8 copy-done.6
  8.2 2.1 scatter_fusion
  10.3 1.3 copy.9
  11.6 7.5 %all-to-all-start = ((bf16[2,1,16,1,128,128]{4,5,0,1,3,2:T(8,128)(2,1)}), bf16[2,1,16,1,128,128]{4,5,0,1,3,2:T(8,128)(2,1)S(1)}, u32[]{:S(2)}, u32[]{:S(2)}) async-start(bf16[2,1,16,1,128,128]{4,5,0,1,3,2:T(8,128)(2,1)} %copy.9), calls=%async_computation | async-start | bytes 2097152 | tf_op jit(solution)/shard_map/all_to_all | solution.py:33
  19.2 0.0 all-gather.5.cloned.1.call-start
  19.2 0.0 copy-done.4
  19.2 0.6 convert_element_type.12
  19.9 0.0 all-gather.5.cloned.1.call-update
  19.9 23.3 %all-to-all-done = bf16[2,1,16,1,128,128]{4,5,0,1,3,2:T(8,128)(2,1)S(1)} async-done(((bf16[2,1,16,1,128,128]{4,5,0,1,3,2:T(8,128)(2,1)}), bf16[2,1,16,1,128,128]{4,5,0,1,3,2:T(8,128)(2,1)S(1)}, u32[]{:S(2)}, u32[]{:S(2)}) %all-to-all-start) | async-done | bytes 1048608 | tf_op jit(solution)/shard_map/all_to_all | solution.py:33
  43.2 1.1 copy.10
  44.3 3.6 %all-to-all-start.1 = ((bf16[2,1,16,1,128,128]{4,5,2,1,3,0:T(8,128)(2,1)}), bf16[2,1,16,1,128,128]{4,5,2,1,3,0:T(8,128)(2,1)S(1)}, u32[]{:S(2)}, u32[]{:S(2)}) async-start(bf16[2,1,16,1,128,128]{4,5,2,1,3,0:T(8,128)(2,1)} %copy.10), calls=%async_computation.1 | async-start | bytes 2097152 | tf_op jit(solution)/shard_map/all_to_all | solution.py:32
  47.9 0.0 reduce-scatter.5.cloned.1.call-start
  48.0 0.1 broadcast_and_fusion
  48.0 14.3 %all-to-all-done.1 = bf16[2,1,16,1,128,128]{4,5,2,1,3,0:T(8,128)(2,1)S(1)} async-done(((bf16[2,1,16,1,128,128]{4,5,2,1,3,0:T(8,128)(2,1)}), bf16[2,1,16,1,128,128]{4,5,2,1,3,0:T(8,128)(2,1)S(1)}, u32[]{:S(2)}, u32[]{:S(2)}) %all-to-all-start.1) | async-done | bytes 1048608 | tf_op jit(solution)/shard_map/all_to_all | solution.py:32
  62.3 0.2 bitcast_add_fusion
  62.5 3.5 %all-gather.5.cloned.1.call-done = bf16[2048,256]{1,0:T(8,128)(2,1)} async-done(((bf16[128,256]{1,0:T(8,128)(2,1)}), bf16[2048,256]{1,0:T(8,128)(2,1)}) %all-gather.5.cloned.1.call-update) | async-done | bytes 1048592 | tf_op jit(solution)/shard_map/all_gather | solution.py:57
  66.0 1.7 convolution_bitcast_fusion.3
  67.6 1.0 fusion.1
  68.6 0.0 copy-start.1
  68.6 0.0 copy-start.7
  68.6 0.7 copy-done.1
  69.3 0.0 reduce-scatter.5.cloned.1.call-update
  69.3 0.0 all-gather.7.cloned.1.call-start
  69.4 0.0 copy-done.7
  69.4 0.6 fusion.38
  73.3 6.9 %reduce-scatter.5.cloned.1.call-done = f32[128,256]{1,0:T(8,128)} async-done(((f32[256,256]{1,0:T(8,128)}), f32[128,256]{1,0:T(8,128)}) %reduce-scatter.5.cloned.1.call-update) | async-done | bytes 131088 | tf_op jit(solution)/shard_map/reduce_scatter | solution.py:71
  80.2 1.6 fusion.37
  81.8 0.0 all-gather.7.cloned.1.call-update
  81.8 0.0 reduce-scatter.7.cloned.1.call-start
  81.8 38.4 %all-gather.7.cloned.1.call-done = bf16[2048,256]{1,0:T(8,128)(2,1)} async-done(((bf16[128,256]{1,0:T(8,128)(2,1)}), bf16[2048,256]{1,0:T(8,128)(2,1)}) %all-gather.7.cloned.1.call-update) | async-done | bytes 1048592 | tf_op jit(solution)/shard_map/all_gather | solution.py:57
  120.3 1.7 convolution_bitcast_fusion.2
  121.9 1.0 fusion.3
  122.9 0.0 copy-start.2
  122.9 0.7 copy-done.2
  123.6 0.0 reduce-scatter.7.cloned.1.call-update
  123.7 0.0 all-gather.9.cloned.1.call-start
  123.9 10.7 %reduce-scatter.7.cloned.1.call-done = f32[128,256]{1,0:T(8,128)} async-done(((f32[256,256]{1,0:T(8,128)}), f32[128,256]{1,0:T(8,128)}) %reduce-scatter.7.cloned.1.call-update) | async-done | bytes 131088 | tf_op jit(solution)/shard_map/reduce_scatter | solution.py:71
  134.6 1.6 fusion.36
  136.1 0.0 all-gather.9.cloned.1.call-update
  136.1 0.0 reduce-scatter.9.cloned.1.call-start
  136.2 38.3 %all-gather.9.cloned.1.call-done = bf16[2048,256]{1,0:T(8,128)(2,1)} async-done(((bf16[128,256]{1,0:T(8,128)(2,1)}), bf16[2048,256]{1,0:T(8,128)(2,1)}) %all-gather.9.cloned.1.call-update) | async-done | bytes 1048592 | tf_op jit(solution)/shard_map/all_gather | solution.py:57
  174.5 1.7 convolution_bitcast_fusion.1
  176.1 1.0 fusion.5
  177.1 0.0 copy-start.3
  177.1 0.7 copy-done.3
  177.8 0.0 reduce-scatter.9.cloned.1.call-update
  177.9 0.0 all-gather.11.cloned.1.call-start
  178.0 10.8 %reduce-scatter.9.cloned.1.call-done = f32[128,256]{1,0:T(8,128)} async-done(((f32[256,256]{1,0:T(8,128)}), f32[128,256]{1,0:T(8,128)}) %reduce-scatter.9.cloned.1.call-update) | async-done | bytes 131088 | tf_op jit(solution)/shard_map/reduce_scatter | solution.py:71
  188.8 1.6 fusion.24
  190.3 0.0 all-gather.11.cloned.1.call-update
  190.3 0.0 reduce-scatter.11.cloned.1.call-start
  190.4 38.4 %all-gather.11.cloned.1.call-done = bf16[2048,256]{1,0:T(8,128)(2,1)} async-done(((bf16[128,256]{1,0:T(8,128)(2,1)}), bf16[2048,256]{1,0:T(8,128)(2,1)}) %all-gather.11.cloned.1.call-update) | async-done | bytes 1048592 | tf_op jit(solution)/shard_map/all_gather | solution.py:57
  228.8 1.7 convolution_bitcast_fusion
  230.5 1.0 fusion.7
  231.5 0.0 copy-start
  231.5 0.7 copy-done
  232.2 0.0 reduce-scatter.11.cloned.1.call-update
  232.3 10.8 %reduce-scatter.11.cloned.1.call-done = f32[128,256]{1,0:T(8,128)} async-done(((f32[256,256]{1,0:T(8,128)}), f32[128,256]{1,0:T(8,128)}) %reduce-scatter.11.cloned.1.call-update) | async-done | bytes 131088 | tf_op jit(solution)/shard_map/reduce_scatter | solution.py:71
  243.1 0.0 copy-done.5
  243.1 1.6 multiply_subtract_fusion
  (7 shorter events, 0.0 us)
Async XLA Ops:
  6.5 0.7 copy-start.8
  6.5 0.7 copy-start.9
  7.2 1.0 copy-start.6
  11.6 7.6 %copy-start.4 = (f32[128,256]{1,0:T(8,128)S(1)}, f32[128,256]{1,0:T(8,128)}, u32[]{:S(2)}) copy-start(f32[128,256]{1,0:T(8,128)} %param.5) | copy-start | bytes 393220
  11.6 31.6 %all-to-all-start = ((bf16[2,1,16,1,128,128]{4,5,0,1,3,2:T(8,128)(2,1)}), bf16[2,1,16,1,128,128]{4,5,0,1,3,2:T(8,128)(2,1)S(1)}, u32[]{:S(2)}, u32[]{:S(2)}) async-start(bf16[2,1,16,1,128,128]{4,5,0,1,3,2:T(8,128)(2,1)} %copy.9), calls=%async_computation | async-start | bytes 2097152 | tf_op jit(solution)/shard_map/all_to_all | solution.py:33
  19.2 46.8 %all-gather.5.cloned.1.call-start = ((), (), s32[]{:S(2)}) async-start(), calls=%async_computation.6 | async-start | bytes 1114112 | tf_op jit(solution)/shard_map/all_gather | solution.py:57
  44.3 18.0 %all-to-all-start.1 = ((bf16[2,1,16,1,128,128]{4,5,2,1,3,0:T(8,128)(2,1)}), bf16[2,1,16,1,128,128]{4,5,2,1,3,0:T(8,128)(2,1)S(1)}, u32[]{:S(2)}, u32[]{:S(2)}) async-start(bf16[2,1,16,1,128,128]{4,5,2,1,3,0:T(8,128)(2,1)} %copy.10), calls=%async_computation.1 | async-start | bytes 2097152 | tf_op jit(solution)/shard_map/all_to_all | solution.py:32
  47.9 32.4 %reduce-scatter.5.cloned.1.call-start = ((), (), s32[]{:S(2)}) async-start(), calls=%async_computation.7 | async-start | bytes 393216 | tf_op jit(solution)/shard_map/reduce_scatter | solution.py:71
  68.6 0.7 copy-start.1
  68.6 0.8 copy-start.7
  69.3 50.9 %all-gather.7.cloned.1.call-start = ((), (), s32[]{:S(2)}) async-start(), calls=%async_computation.8 | async-start | bytes 1114112 | tf_op jit(solution)/shard_map/all_gather | solution.py:57
  81.8 52.8 %reduce-scatter.7.cloned.1.call-start = ((), (), s32[]{:S(2)}) async-start(), calls=%async_computation.9 | async-start | bytes 393216 | tf_op jit(solution)/shard_map/reduce_scatter | solution.py:71
  122.9 0.7 copy-start.2
  123.7 50.8 %all-gather.9.cloned.1.call-start = ((), (), s32[]{:S(2)}) async-start(), calls=%async_computation.10 | async-start | bytes 1114112 | tf_op jit(solution)/shard_map/all_gather | solution.py:57
  136.1 52.6 %reduce-scatter.9.cloned.1.call-start = ((), (), s32[]{:S(2)}) async-start(), calls=%async_computation.11 | async-start | bytes 393216 | tf_op jit(solution)/shard_map/reduce_scatter | solution.py:71
  177.1 0.7 copy-start.3
  177.9 51.0 %all-gather.11.cloned.1.call-start = ((), (), s32[]{:S(2)}) async-start(), calls=%async_computation.12 | async-start | bytes 1114112 | tf_op jit(solution)/shard_map/all_gather | solution.py:57
  190.3 52.8 %reduce-scatter.11.cloned.1.call-start = ((), (), s32[]{:S(2)}) async-start(), calls=%async_computation.13 | async-start | bytes 393216 | tf_op jit(solution)/shard_map/reduce_scatter | solution.py:71
  231.5 0.7 copy-start
  231.5 11.6 %copy-start.5 = (f32[128,256]{1,0:T(8,128)S(1)}, f32[128,256]{1,0:T(8,128)}, u32[]{:S(2)}) copy-start(f32[128,256]{1,0:T(8,128)} %reduce-scatter.9.cloned.1.call-done) | copy-start | bytes 393220
Sparse Core Ops, SparseCore 0:
  22.2 43.7 all-gather.4
  69.5 10.6 reduce-scatter.4
  82.4 37.8 all-gather.6
  123.8 10.7 reduce-scatter.6
  136.6 37.8 all-gather.8
  178.0 10.7 reduce-scatter.8
  190.9 37.8 all-gather.10
  232.3 10.7 reduce-scatter.10
where the time goes:
time: 252 us
  waiting for transfers between devices  195 us (77%)
  between operations  17.3 us (7%)
  starting transfers between devices  11.5 us (5%)
  matrix products  10.6 us (4%)
  other arithmetic  9.26 us (4%)
  local copies, waits for them, and re-layouts  7.5 us (3%)
    all_gather x4, waiting for transfers between devices, apply_matrix(): lax.all_gather(low_vectors, 'row', axis=0, tiled=True)  119 us
    reduce_scatter x4, waiting for transfers between devices, apply_matrix(): lax.psum_scatter(near_partial.reshape(near_count * tile_size, vec_width),...  39.2 us
    all_to_all x1, waiting for transfers between devices, local(): lax.all_to_all(owned, 'row', split_axis=2, concat_axis=2, tiled=True)  23.3 us
    all_to_all x1, waiting for transfers between devices, local(): lax.all_to_all(lax.all_to_all(owned, 'row', split_axis=2, concat_axis=2,...  14.3 us
    all_to_all x1, starting transfers between devices, local(): lax.all_to_all(owned, 'row', split_axis=2, concat_axis=2, tiled=True)  7.55 us
    dot_general x4, matrix products, apply_matrix(): jnp.einsum('apxy,pyk->axk', window, far_vectors, preferred_element_type=j...  6.63 us
    convert_element_type x4, other arithmetic, apply_matrix(): low_vectors = vectors.astype(jnp.bfloat16)  5.32 us
  transfers between devices with their start and end apart: 10, of which 10 were waited for; matrix products, arithmetic and copies ran while one was open for 1% of the time, Pallas kernels for 0%

commit v1 on v0

--- a/solution.py
+++ b/solution.py
@@ -1,9 +1,21 @@
+import functools
 import jax
 import jax.numpy as jnp
 from jax import lax
 from jax.sharding import PartitionSpec as P
 
 DEGREE = 4
+
+
+def feed_levels_all(z, in_dim, array_dim):
+    before = lax.axis_size("row")
+    w2 = jnp.split(z, before, in_dim)
+    upper = jnp.stack(w2, 0)
+    h_now = lax.all_to_all(upper, "row", 0, 0)
+    return jnp.concatenate(h_now, axis=array_dim)
+
+
+unite_rings = functools.partial(feed_levels_all, in_dim=2, array_dim=2)
 
 
 def local(start_block, tiles, tile_rows, tile_cols, bounds):
@@ -29,13 +41,7 @@
     owned = jnp.zeros((near_count * far_count, tile_size, tile_size), jnp.bfloat16)
     owned = owned.at[slot_place].add(tile_mats, mode="drop")
     owned = owned.reshape(col_count, blocks, row_count, blocks, tile_size, tile_size)
-    received = lax.all_to_all(
-        lax.all_to_all(owned, "row", split_axis=2, concat_axis=2, tiled=True),
-        "col",
-        split_axis=0,
-        concat_axis=0,
-        tiled=True,
-    )
+    received = lax.all_to_all(unite_rings(owned), "col", split_axis=0, concat_axis=0, tiled=True)
     mirror = jnp.transpose(received, (0, 3, 2, 1, 5, 4))
     grid_shape = (col_count, blocks, row_count, blocks)
     col_grid = lax.broadcasted_iota(jnp.int32, grid_shape, 0)

time: 252 us -> 262 us (1.040)
  local copies, waits for them, and re-layouts: 7.5 us -> 16.9 us
    unnamed x20 -> x35, local copies, waits for them, and re-layouts: 4.23 us -> 13.7 us
where the time goes in v1:
time: 262 us; the launch traced here: 261 us
  waiting for transfers between devices  195 us (74%)
  between operations  17.3 us (7%)
  local copies, waits for them, and re-layouts  16.9 us (6%)
  starting transfers between devices  11.5 us (4%)
  matrix products  10.6 us (4%)
  other arithmetic  9.26 us (4%)
    all_gather x4, waiting for transfers between devices, apply_matrix(): lax.all_gather(low_vectors, 'row', axis=0, tiled=True)  118 us
    reduce_scatter x4, waiting for transfers between devices, apply_matrix(): lax.psum_scatter(near_partial.reshape(near_count * tile_size, vec_width),...  39.7 us
    all_to_all x1, waiting for transfers between devices, feed_levels_all(): h_now = lax.all_to_all(upper, 'row', 0, 0)  23.3 us
    all_to_all x1, waiting for transfers between devices, local(): lax.all_to_all(unite_rings(owned), 'col', split_axis=0, concat_axis=0, ti...  14.3 us
    unnamed x35, local copies, waits for them, and re-layouts  13.7 us
    all_to_all x1, starting transfers between devices, feed_levels_all(): h_now = lax.all_to_all(upper, 'row', 0, 0)  7.55 us
    dot_general x4, matrix products, apply_matrix(): jnp.einsum('apxy,pyk->axk', window, far_vectors, preferred_element_type=j...  6.63 us
    convert_element_type x4, other arithmetic, apply_matrix(): low_vectors = vectors.astype(jnp.bfloat16)  5.32 us
  transfers between devices with their start and end apart: 10, of which 10 were waited for; matrix products, arithmetic and copies ran while one was open for 1% of the time, Pallas kernels for 0%

profile of v1, /device:TPU:0, one launch (start us, length us, event | category | flops | bytes accessed | tf_op | source)
XLA Modules:
  0.0 260.8 jit_solution(9959051007246926803)
XLA Ops:
  6.5 0.7 copy-done.8
  7.2 0.2 broadcast_in_dim.27
  7.5 0.8 copy-done.6
  8.2 2.1 scatter_fusion
  10.3 0.6 fusion.27
  11.0 0.6 fusion.26
  11.6 0.6 fusion.25
  12.2 0.6 fusion.24
  12.8 0.6 fusion.23
  13.5 0.6 fusion.22
  14.1 0.6 fusion.21
  14.7 0.6 fusion.20
  15.4 0.6 fusion.19
  16.0 0.6 fusion.18
  16.6 0.6 fusion.17
  17.3 0.6 fusion.16
  17.9 0.6 fusion.15
  18.5 0.6 fusion.14
  19.2 0.6 fusion.13
  19.8 0.6 fusion.12
  20.4 7.5 %all-to-all-start = ((bf16[16,2,1,1,1,128,128]{6,5,1,4,3,2,0:T(8,128)(2,1)}), bf16[16,2,1,1,1,128,128]{6,5,1,4,3,2,0:T(8,128)(2,1)S(1)}, u32[]{:S(2)}, u32[]{:S(2)}) async-start(bf16[16,2,1,1,1,128,128]{6,5,1,4,3,2,0:T(8,128)(2,1)} %fusion.12), calls=%async_computation | async-start | bytes 2097152 | tf_op jit(solution)/shard_map/all_to_all | solution.py:14
  28.0 0.0 all-gather.5.cloned.1.call-start
  28.0 0.6 convert_element_type.12
  28.7 0.0 all-gather.5.cloned.1.call-update
  28.7 23.3 %all-to-all-done = bf16[16,2,1,1,1,128,128]{6,5,1,4,3,2,0:T(8,128)(2,1)S(1)} async-done(((bf16[16,2,1,1,1,128,128]{6,5,1,4,3,2,0:T(8,128)(2,1)}), bf16[16,2,1,1,1,128,128]{6,5,1,4,3,2,0:T(8,128)(2,1)S(1)}, u32[]{:S(2)}, u32[]{:S(2)}) %all-to-all-start) | async-done | bytes 1048608 | tf_op jit(solution)/shard_map/all_to_all | solution.py:14
  52.0 1.1 copy.57
  53.1 3.6 %all-to-all-start.1 = ((bf16[2,1,16,1,128,128]{5,4,2,3,1,0:T(8,128)(2,1)}), bf16[2,1,16,1,128,128]{5,4,2,3,1,0:T(8,128)(2,1)S(1)}, u32[]{:S(2)}, u32[]{:S(2)}) async-start(bf16[2,1,16,1,128,128]{5,4,2,3,1,0:T(8,128)(2,1)} %copy.57), calls=%async_computation.1 | async-start | bytes 2097152 | tf_op jit(solution)/shard_map/all_to_all | solution.py:44
  56.6 0.0 reduce-scatter.5.cloned.1.call-start
  56.7 0.1 broadcast_and_fusion
  56.8 14.3 %all-to-all-done.1 = bf16[2,1,16,1,128,128]{5,4,2,3,1,0:T(8,128)(2,1)S(1)} async-done(((bf16[2,1,16,1,128,128]{5,4,2,3,1,0:T(8,128)(2,1)}), bf16[2,1,16,1,128,128]{5,4,2,3,1,0:T(8,128)(2,1)S(1)}, u32[]{:S(2)}, u32[]{:S(2)}) %all-to-all-start.1) | async-done | bytes 1048608 | tf_op jit(solution)/shard_map/all_to_all | solution.py:44
  71.1 0.7 copy.58
  71.8 0.2 bitcast_add_fusion
  71.9 2.8 %all-gather.5.cloned.1.call-done = bf16[2048,256]{1,0:T(8,128)(2,1)} async-done(((bf16[128,256]{1,0:T(8,128)(2,1)}), bf16[2048,256]{1,0:T(8,128)(2,1)}) %all-gather.5.cloned.1.call-update) | async-done | bytes 1048592 | tf_op jit(solution)/shard_map/all_gather | solution.py:63
  74.7 1.7 convolution_bitcast_fusion.3
  76.4 1.0 fusion.1
  77.4 0.7 copy-done.1
  78.1 0.0 reduce-scatter.5.cloned.1.call-update
  78.1 0.0 all-gather.7.cloned.1.call-start
  78.2 0.6 fusion.54
  82.1 7.4 %reduce-scatter.5.cloned.1.call-done = f32[128,256]{1,0:T(8,128)} async-done(((f32[256,256]{1,0:T(8,128)}), f32[128,256]{1,0:T(8,128)}) %reduce-scatter.5.cloned.1.call-update) | async-done | bytes 131088 | tf_op jit(solution)/shard_map/reduce_scatter | solution.py:77
  89.5 1.6 fusion.53
  91.0 0.0 reduce-scatter.7.cloned.1.call-start
  91.1 38.4 %all-gather.7.cloned.1.call-done = bf16[2048,256]{1,0:T(8,128)(2,1)} async-done(((bf16[128,256]{1,0:T(8,128)(2,1)}), bf16[2048,256]{1,0:T(8,128)(2,1)}) %all-gather.7.cloned.1.call-update) | async-done | bytes 1048592 | tf_op jit(solution)/shard_map/all_gather | solution.py:63
  129.5 1.7 convolution_bitcast_fusion.2
  131.2 1.0 fusion.3
  132.2 0.7 copy-done.2
  132.9 0.0 all-gather.9.cloned.1.call-start
  133.2 10.7 %reduce-scatter.7.cloned.1.call-done = f32[128,256]{1,0:T(8,128)} async-done(((f32[256,256]{1,0:T(8,128)}), f32[128,256]{1,0:T(8,128)}) %reduce-scatter.7.cloned.1.call-update) | async-done | bytes 131088 | tf_op jit(solution)/shard_map/reduce_scatter | solution.py:77
  143.8 1.6 fusion.52
  145.4 0.0 reduce-scatter.9.cloned.1.call-start
  145.5 38.3 %all-gather.9.cloned.1.call-done = bf16[2048,256]{1,0:T(8,128)(2,1)} async-done(((bf16[128,256]{1,0:T(8,128)(2,1)}), bf16[2048,256]{1,0:T(8,128)(2,1)}) %all-gather.9.cloned.1.call-update) | async-done | bytes 1048592 | tf_op jit(solution)/shard_map/all_gather | solution.py:63
  183.7 1.7 convolution_bitcast_fusion.1
  185.4 1.0 fusion.5
  186.4 0.7 copy-done.3
  187.1 0.0 all-gather.11.cloned.1.call-start
  187.3 10.8 %reduce-scatter.9.cloned.1.call-done = f32[128,256]{1,0:T(8,128)} async-done(((f32[256,256]{1,0:T(8,128)}), f32[128,256]{1,0:T(8,128)}) %reduce-scatter.9.cloned.1.call-update) | async-done | bytes 131088 | tf_op jit(solution)/shard_map/reduce_scatter | solution.py:77
  198.0 1.6 fusion.40
  199.6 0.0 reduce-scatter.11.cloned.1.call-start
  199.7 38.4 %all-gather.11.cloned.1.call-done = bf16[2048,256]{1,0:T(8,128)(2,1)} async-done(((bf16[128,256]{1,0:T(8,128)(2,1)}), bf16[2048,256]{1,0:T(8,128)(2,1)}) %all-gather.11.cloned.1.call-update) | async-done | bytes 1048592 | tf_op jit(solution)/shard_map/all_gather | solution.py:63
  238.1 1.7 convolution_bitcast_fusion
  239.8 1.0 fusion.7
  240.8 0.7 copy-done
  241.6 10.8 %reduce-scatter.11.cloned.1.call-done = f32[128,256]{1,0:T(8,128)} async-done(((f32[256,256]{1,0:T(8,128)}), f32[128,256]{1,0:T(8,128)}) %reduce-scatter.11.cloned.1.call-update) | async-done | bytes 131088 | tf_op jit(solution)/shard_map/reduce_scatter | solution.py:77
  252.4 1.6 multiply_subtract_fusion
  (23 shorter events, 0.2 us)
Async XLA Ops:
  6.5 0.7 copy-start.8
  6.5 0.7 copy-start.9
  7.2 1.0 copy-start.6
  20.4 7.6 %copy-start.4 = (f32[128,256]{1,0:T(8,128)S(1)}, f32[128,256]{1,0:T(8,128)}, u32[]{:S(2)}) copy-start(f32[128,256]{1,0:T(8,128)} %param.5) | copy-start | bytes 393220
  20.4 31.6 %all-to-all-start = ((bf16[16,2,1,1,1,128,128]{6,5,1,4,3,2,0:T(8,128)(2,1)}), bf16[16,2,1,1,1,128,128]{6,5,1,4,3,2,0:T(8,128)(2,1)S(1)}, u32[]{:S(2)}, u32[]{:S(2)}) async-start(bf16[16,2,1,1,1,128,128]{6,5,1,4,3,2,0:T(8,128)(2,1)} %fusion.12), calls=%async_computation | async-start | bytes 2097152 | tf_op jit(solution)/shard_map/all_to_all | solution.py:14
  28.0 46.8 %all-gather.5.cloned.1.call-start = ((), (), s32[]{:S(2)}) async-start(), calls=%async_computation.6 | async-start | bytes 1114112 | tf_op jit(solution)/shard_map/all_gather | solution.py:63
  53.1 18.0 %all-to-all-start.1 = ((bf16[2,1,16,1,128,128]{5,4,2,3,1,0:T(8,128)(2,1)}), bf16[2,1,16,1,128,128]{5,4,2,3,1,0:T(8,128)(2,1)S(1)}, u32[]{:S(2)}, u32[]{:S(2)}) async-start(bf16[2,1,16,1,128,128]{5,4,2,3,1,0:T(8,128)(2,1)} %copy.57), calls=%async_computation.1 | async-start | bytes 2097152 | tf_op jit(solution)/shard_map/all_to_all | solution.py:44
  56.6 32.8 %reduce-scatter.5.cloned.1.call-start = ((), (), s32[]{:S(2)}) async-start(), calls=%async_computation.7 | async-start | bytes 393216 | tf_op jit(solution)/shard_map/reduce_scatter | solution.py:77
  77.4 0.7 copy-start.1
  77.4 0.8 copy-start.7
  78.1 51.4 %all-gather.7.cloned.1.call-start = ((), (), s32[]{:S(2)}) async-start(), calls=%async_computation.8 | async-start | bytes 1114112 | tf_op jit(solution)/shard_map/all_gather | solution.py:63
  91.0 52.8 %reduce-scatter.7.cloned.1.call-start = ((), (), s32[]{:S(2)}) async-start(), calls=%async_computation.9 | async-start | bytes 393216 | tf_op jit(solution)/shard_map/reduce_scatter | solution.py:77
  132.2 0.7 copy-start.2
  132.9 50.8 %all-gather.9.cloned.1.call-start = ((), (), s32[]{:S(2)}) async-start(), calls=%async_computation.10 | async-start | bytes 1114112 | tf_op jit(solution)/shard_map/all_gather | solution.py:63
  145.4 52.6 %reduce-scatter.9.cloned.1.call-start = ((), (), s32[]{:S(2)}) async-start(), calls=%async_computation.11 | async-start | bytes 393216 | tf_op jit(solution)/shard_map/reduce_scatter | solution.py:77
  186.4 0.7 copy-start.3
  187.1 51.0 %all-gather.11.cloned.1.call-start = ((), (), s32[]{:S(2)}) async-start(), calls=%async_computation.12 | async-start | bytes 1114112 | tf_op jit(solution)/shard_map/all_gather | solution.py:63
  199.6 52.8 %reduce-scatter.11.cloned.1.call-start = ((), (), s32[]{:S(2)}) async-start(), calls=%async_computation.13 | async-start | bytes 393216 | tf_op jit(solution)/shard_map/reduce_scatter | solution.py:77
  240.8 0.7 copy-start
  240.8 11.6 %copy-start.5 = (f32[128,256]{1,0:T(8,128)S(1)}, f32[128,256]{1,0:T(8,128)}, u32[]{:S(2)}) copy-start(f32[128,256]{1,0:T(8,128)} %reduce-scatter.9.cloned.1.call-done) | copy-start | bytes 393220
Sparse Core Ops, SparseCore 0:
  30.9 43.7 all-gather.4
  78.3 11.1 reduce-scatter.4
  91.6 37.8 all-gather.6
  133.1 10.7 reduce-scatter.6
  145.8 37.8 all-gather.8
  187.3 10.7 reduce-scatter.8
  200.2 37.8 all-gather.10
  241.6 10.7 reduce-scatter.10
